TPU v7x, 32 devices: a whole 2x2x4 slice. The times are simulated.
32 devices in a mesh: ctx: 2 (over y), exp: 16 (over z, x, core).
Axes of the slice: x: 2, y: 2, z: 4, core: 2. Of those that a mesh axis runs over, the one named last changes fastest.
Arguments:
- residual: bfloat16 [16, 128, 2048], P('exp', 'ctx'), may hold values from -1 to 1
- queries: bfloat16 [16, 128, 2048], P('exp', 'ctx'), may hold values from -6 to 6
- key_rows: bfloat16 [16, 128, 256], P('exp', 'ctx'), may hold values from -6 to 6
- value_rows: bfloat16 [16, 128, 256], P('exp', 'ctx'), may hold values from -0.8984375 to 0.8984375
- span_order: int32 [4], replicated, may hold values from 0 to 3, as said below
- norm_gain: float32 [2048], replicated, may hold values from 0.1 to 1.9
- gate_logits: float32 [16, 128, 8], P('exp', 'ctx'), may hold values from -6 to 6
- expert_ids: int32 [16, 128, 8], P('exp', 'ctx'), may hold values from 0 to 15, all different within a row; in each aligned block of 64 rows (0 to 63, 64 to 127, ..., all dimensions but the last counted through in order) at most 32 rows name the same one
- gate_up: bfloat16 [16, 2048, 768], P('exp'), may hold values from -1 to 1
- down_weight: bfloat16 [16, 384, 2048], P('exp'), may hold values from -0.3125 to 0.3125
Outputs:
- layer_out: bfloat16 [16, 128, 2048], P('exp', 'ctx')
Inputs may be any that keep to these rules, and one draw needn't show every extreme that they name: A permutation of 0 to 3; rows b * 32 to b * 32 + 31 of every sequence hold positions span_order[b] * 32 onward. `expert_ids`: each token names 8 different experts; within the 64 rows of one device (aligned blocks of rows) no expert is named by more than 32 tokens.
All inputs are finite; a program needn't handle non-finite values.
Results may differ from a plain program's by a relative error of at most 0.0062.
Values may be sent and summed in bfloat16 or wider, within the bound.
A program may use at most 64 MiB of HBM per device.

v0:
```python
import math
import jax
import jax.numpy as jnp
from jax import lax
from jax.sharding import PartitionSpec as P

KVH = 2
HD = 128
GROUP = 8
HALF = 32
big_negative = -1e30
norm_eps = 1e-06


def span_positions(span_order, first_row, row_total):
    row_index = first_row + jnp.arange(row_total, dtype=jnp.int32)
    onehot = (row_index // HALF)[:, None] == jnp.arange(span_order.shape[0], dtype=jnp.int32)[
        None, :
    ]
    block_start = jnp.sum(jnp.where(onehot, span_order[None, :], 0), axis=1)
    return block_start * HALF + row_index % HALF


def attend_update(state_in, pieces, first_index, query_heads, query_pos, span_order):
    running_max, running_sum, running_out = state_in
    key_piece, value_piece = pieces
    key_count = key_piece.shape[1]
    key_heads = key_piece[0].reshape(key_count, KVH, HD)
    value_heads = value_piece[0].reshape(key_count, KVH, HD)
    key_pos = span_positions(span_order, first_index, key_count)
    score_scale = 1.0 / math.sqrt(HD)
    scores = (
        jnp.einsum("tgqd,cgd->gqtc", query_heads, key_heads, preferred_element_type=jnp.float32)
        * score_scale
    )
    visible = (key_pos[None, :] <= query_pos[:, None])[None, None]
    scores = jnp.where(visible, scores, big_negative)
    new_max = jnp.maximum(running_max, jnp.max(scores, axis=3))
    weights = jnp.where(visible, jnp.exp(scores - new_max[..., None]), 0.0)
    new_sum = jnp.sum(weights, axis=3)
    product = jnp.einsum(
        "gqtc,cgd->tgqd",
        weights.astype(jnp.bfloat16),
        value_heads,
        preferred_element_type=jnp.float32,
    )
    return (new_max, new_sum, product)


def run_expert(arrived, gate_up, down_weight):
    sources, slots, width = arrived.shape
    rows_in = arrived.reshape(sources * slots, width)
    projected = jnp.dot(rows_in, gate_up[0], preferred_element_type=jnp.float32)
    hidden_units = gate_up.shape[2] // 2
    hidden = (jax.nn.silu(projected[:, :hidden_units]) * projected[:, hidden_units:]).astype(
        jnp.bfloat16
    )
    result = jnp.dot(hidden, down_weight[0], preferred_element_type=jnp.float32).astype(
        jnp.bfloat16
    )
    return result.reshape(sources, slots, width)


def local(
    residual,
    queries,
    key_rows,
    value_rows,
    span_order,
    norm_gain,
    gate_logits,
    expert_ids,
    gate_up,
    down_weight,
):
    tokens_here = residual.shape[1]
    model_width = residual.shape[2]
    ctx_index = lax.axis_index("ctx")
    query_pos = span_positions(span_order, ctx_index * tokens_here, tokens_here)
    query_heads = queries[0].reshape(tokens_here, KVH, GROUP, HD)
    state_shape = (KVH, GROUP, tokens_here)
    initial = (
        jnp.full(state_shape, big_negative, jnp.float32),
        jnp.zeros(state_shape, jnp.float32),
        jnp.zeros((tokens_here, KVH, GROUP, HD), jnp.float32),
    )
    final_state = attend_update(
        initial,
        (
            lax.all_gather(key_rows, "ctx", axis=1, tiled=True),
            lax.all_gather(value_rows, "ctx", axis=1, tiled=True),
        ),
        jnp.int32(0),
        query_heads,
        query_pos,
        span_order,
    )
    running_sum = final_state[1]
    attention = (final_state[2] / jnp.transpose(running_sum, (2, 0, 1))[..., None]).reshape(
        tokens_here, -1
    )
    attention = lax.optimization_barrier(attention.astype(jnp.bfloat16)).astype(jnp.float32)
    mixed_rows = residual[0].astype(jnp.float32) + attention
    scale_rms = lax.rsqrt(jnp.mean(mixed_rows * mixed_rows, axis=1, keepdims=True) + norm_eps)
    normed = (mixed_rows * scale_rms * norm_gain).astype(jnp.bfloat16)
    raised = jnp.exp(gate_logits[0])
    routing_weight = raised / jnp.sum(raised, axis=1, keepdims=True)
    destinations = lax.axis_size("exp")
    top_count = expert_ids.shape[2]
    mean_load = tokens_here * top_count // destinations
    with_slack = mean_load + tokens_here * top_count // (4 * destinations)
    capacity = min(
        tokens_here, max(2, max(mean_load, min(with_slack, 524288 // (destinations * model_width))))
    )
    flat_experts = expert_ids[0].reshape(-1)
    owner_onehot = (
        flat_experts[:, None] == jnp.arange(destinations, dtype=jnp.int32)[None, :]
    ).astype(jnp.int32)
    earlier = jnp.cumsum(owner_onehot, axis=0) - owner_onehot
    slot_rank = jnp.sum(earlier * owner_onehot, axis=1)
    target_slot = flat_experts * capacity + slot_rank
    placement = (
        target_slot[:, None] == jnp.arange(destinations * capacity, dtype=jnp.int32)[None, :]
    ).astype(jnp.int32)
    token_map = placement.reshape(tokens_here, top_count, -1).sum(axis=1).astype(jnp.bfloat16)
    outgoing = jnp.einsum(
        "ts,td->sd", token_map, normed, preferred_element_type=jnp.float32
    ).astype(jnp.bfloat16)
    outgoing = outgoing.reshape(destinations, capacity, -1)
    arrived = lax.all_to_all(outgoing, "exp", split_axis=0, concat_axis=0, tiled=True)
    returned = lax.all_to_all(
        run_expert(arrived, gate_up, down_weight), "exp", split_axis=0, concat_axis=0, tiled=True
    )
    returned_rows = returned.reshape(destinations * capacity, -1)
    picked = (
        jnp.take(returned_rows, target_slot, axis=0)
        .astype(jnp.float32)
        .reshape(tokens_here, top_count, -1)
    )
    combined = jnp.sum(picked * routing_weight[:, :, None], axis=1)
    layer_out = (mixed_rows + combined).astype(jnp.bfloat16)
    return layer_out[None]


def solution(mesh):
    return jax.shard_map(
        local,
        mesh=mesh,
        in_specs=(
            P("exp", "ctx", None),
            P("exp", "ctx", None),
            P("exp", "ctx", None),
            P("exp", "ctx", None),
            P(),
            P(),
            P("exp", "ctx", None),
            P("exp", "ctx", None),
            P("exp", None, None),
            P("exp", None, None),
        ),
        out_specs=P("exp", "ctx", None),
        check_vma=False,
    )
```

profile of v0, /device:TPU:11, one launch (start us, length us, event | category | flops | bytes accessed | tf_op | source)
XLA Modules:
  0.0 144.3 jit_solution(2318185665745731534)
XLA Ops:
  0.0 0.9 copy.54
  1.1 0.7 select_reduce_fusion
  1.9 0.7 select_reduce_fusion.1
  2.6 1.0 copy.69
  3.6 3.6 %all_gather.6 = bf16[1,128,256]{2,1,0:T(8,128)(2,1)S(1)} all-gather(bf16[1,64,256]{2,1,0:T(8,128)(2,1)} %param.12), channel_id=1, replica_groups=mesh['ctx'=2,'exp'=16] {'ctx'}, dimensions={1}, use_global_device_ids=true | all-gather | bytes 98304 | tf_op jit(solution)/shard_map/all_gather | solution.py:90
  7.5 1.0 fusion.30
  8.5 3.6 %all_gather.7 = bf16[1,128,256]{2,1,0:T(8,128)(2,1)S(1)} all-gather(bf16[1,64,256]{2,1,0:T(8,128)(2,1)} %param.13), channel_id=1, replica_groups=mesh['ctx'=2,'exp'=16] {'ctx'}, dimensions={1}, use_global_device_ids=true | all-gather | bytes 98304 | tf_op jit(solution)/shard_map/all_gather | solution.py:91
  12.1 0.1 copy.51
  12.2 1.5 %fusion.8 = f32[2,8,64]{2,1,0:T(8,128)S(1)} fusion(f32[2,8,64,128]{3,2,1,0:T(8,128)} %get-tuple-element.8, f32[2,8,64]{2,1,0:T(8,128)S(1)} %broadcast_maximum_fusion, pred[64,128]{1,0:T(8,128)(4,1)S(1)} %broadcast_compare_fusion), kind=kLoop, calls=%fused_computation.23 | loop fusion | flops 392192 | bytes 540672 | tf_op jit(solution)/shard_map/reduce_sum | solution.py:40
  13.8 1.4 fusion.6
  15.2 0.2 copy.53
  15.4 0.2 multiply_reduce_fusion.1
  15.7 1.2 reduce-window.6
  16.8 0.2 slice_reduce_fusion
  17.4 0.4 convert_reduce_fusion
  17.8 1.7 %convolution_convert_fusion.1 = bf16[512,2048]{1,0:T(8,128)(2,1)S(1)} fusion(bf16[64,2048]{1,0:T(8,128)(2,1)S(1)} %bitcast.85, bf16[1,64,2048]{2,1,0:T(8,128)(2,1)} %param.10, f32[2048]{0:T(1024)S(1)} %copy-done.5, f32[64]{0:T(128)S(1)} %add_rsqrt_fusion, s32[64,512]{1,0:T(8,128)S(1)} %convert_reduce_fusion), kind=kOutput, calls=%fused_computation.5 | convolution fusion | flops 136085504 | bytes 2760960 | tf_op jit(solution)/shard_map/ts,td->sd/dot_general | solution.py:126
  19.5 55.9 %all_to_all.10 = bf16[16,32,2048]{2,1,0:T(8,128)(2,1)S(1)} all-to-all(bf16[16,32,2048]{2,1,0:T(8,128)(2,1)S(1)} %bitcast.83), channel_id=1, replica_groups=mesh['ctx'=2,'exp'=16] {'exp'}, dimensions={0} | all-to-all | bytes 4194304 | tf_op jit(solution)/shard_map/all_to_all | solution.py:130
  75.4 1.8 %fusion = f32[512,768]{1,0:T(8,128)S(1)} fusion(bf16[512,2048]{1,0:T(8,128)(2,1)S(1)} %bitcast.88, bf16[1,2048,768]{2,1,0:T(8,128)(2,1)S(1)} %copy-done), kind=kOutput, calls=%fused_computation.2 | convolution fusion | flops 1610612736 | bytes 6815744 | tf_op jit(solution)/shard_map/dot_general | solution.py:53
  77.2 2.6 %convolution_convert_fusion = bf16[512,2048]{1,0:T(8,128)(2,1)} fusion(bf16[1,384,2048]{2,1,0:T(8,128)(2,1)S(1)} %copy-done.6, f32[512,768]{1,0:T(8,128)S(1)} %fusion), kind=kOutput, calls=%fused_computation.4 | convolution fusion | flops 807534592 | bytes 5242880 | tf_op jit(solution)/shard_map/dot_general | solution.py:58
  79.8 5.2 %all-to-all-start.1 = ((bf16[16,32,2048]{2,1,0:T(8,128)(2,1)}), bf16[16,32,2048]{2,1,0:T(8,128)(2,1)}, u32[]{:S(2)}, u32[]{:S(2)}) async-start(bf16[16,32,2048]{2,1,0:T(8,128)(2,1)} %bitcast.87), calls=%async_computation.1 | async-start | bytes 4194304 | tf_op jit(solution)/shard_map/all_to_all | solution.py:131
  85.4 47.1 %all-to-all-done.1 = bf16[16,32,2048]{2,1,0:T(8,128)(2,1)} async-done(((bf16[16,32,2048]{2,1,0:T(8,128)(2,1)}), bf16[16,32,2048]{2,1,0:T(8,128)(2,1)}, u32[]{:S(2)}, u32[]{:S(2)}) %all-to-all-start.1) | async-done | bytes 2097184 | tf_op jit(solution)/shard_map/all_to_all | solution.py:131
  132.5 7.1 %gather_fusion = bf16[512,2048]{1,0:T(8,128)(2,1)} fusion(bf16[512,2048]{1,0:T(8,128)(2,1)} %bitcast.15, s32[1024]{0:T(1024)S(1)} %pad_clamp_fusion), kind=kCustom, calls=%fused_computation | custom fusion | bytes 4196352 | tf_op jit(solution)/shard_map/jit(_take)/gather | solution.py:136
  139.6 3.9 %multiply_reduce_fusion = f32[64,2048]{1,0:T(8,128)S(1)} fusion(bf16[512,2048]{1,0:T(8,128)(2,1)} %gather_fusion, f32[64,8]{1,0:T(8,128)S(1)} %copy.61, pred[64,8]{1,0:T(8,128)(4,1)S(1)} %copy.58), kind=kLoop, calls=%fused_computation.1 | loop fusion | flops 4063232 | bytes 2624000 | tf_op jit(solution)/shard_map/reduce_sum | solution.py:140
  143.5 0.8 fusion.13
  (42 shorter events, 1.3 us)
Async XLA Ops:
  0.0 75.4 %copy-start = (bf16[1,2048,768]{2,1,0:T(8,128)(2,1)S(1)}, bf16[1,2048,768]{2,1,0:T(8,128)(2,1)}, u32[]{:S(2)}) copy-start(bf16[1,2048,768]{2,1,0:T(8,128)(2,1)} %param.18) | copy-start | bytes 9437188
  12.2 3.2 %copy-start.1 = (bf16[1,64,2048]{2,1,0:T(8,128)(2,1)S(1)}, bf16[1,64,2048]{2,1,0:T(8,128)(2,1)}, u32[]{:S(2)}) copy-start(bf16[1,64,2048]{2,1,0:T(8,128)(2,1)} %param.10) | copy-start | bytes 786436
  13.7 3.6 %copy-start.3 = (s32[1,64,8]{1,2,0:T(8,128)S(1)}, s32[1,64,8]{1,2,0:T(8,128)}, u32[]{:S(2)}) copy-start(s32[1,64,8]{1,2,0:T(8,128)} %param.17) | copy-start | bytes 6148
  13.8 4.1 %copy-start.5 = (f32[2048]{0:T(1024)S(1)}, f32[2048]{0:T(1024)}, u32[]{:S(2)}) copy-start(f32[2048]{0:T(1024)} %param.15) | copy-start | bytes 24580
  75.4 1.8 %copy-start.6 = (bf16[1,384,2048]{2,1,0:T(8,128)(2,1)S(1)}, bf16[1,384,2048]{2,1,0:T(8,128)(2,1)}, u32[]{:S(2)}) copy-start(bf16[1,384,2048]{2,1,0:T(8,128)(2,1)} %param.19) | copy-start | bytes 4718596
  79.8 5.5 %copy-start.4 = (f32[1,64,8]{1,2,0:T(8,128)S(1)}, f32[1,64,8]{1,2,0:T(8,128)}, u32[]{:S(2)}) copy-start(f32[1,64,8]{1,2,0:T(8,128)} %param.16) | copy-start | bytes 6148
  79.8 52.7 %all-to-all-start.1 = ((bf16[16,32,2048]{2,1,0:T(8,128)(2,1)}), bf16[16,32,2048]{2,1,0:T(8,128)(2,1)}, u32[]{:S(2)}, u32[]{:S(2)}) async-start(bf16[16,32,2048]{2,1,0:T(8,128)(2,1)} %bitcast.87), calls=%async_computation.1 | async-start | bytes 4194304 | tf_op jit(solution)/shard_map/all_to_all | solution.py:131
  139.6 3.9 %copy-start.2 = (bf16[1,64,2048]{2,1,0:T(8,128)(2,1)S(1)}, bf16[1,64,2048]{2,1,0:T(8,128)(2,1)}, u32[]{:S(2)}) copy-start(bf16[1,64,2048]{2,1,0:T(8,128)(2,1)} %param.10) | copy-start | bytes 786436
where the time goes:
time: 145 us; the launch traced here: 144 us
  blocking collectives  63.2 us (44%)
  waiting for transfers between devices  47.1 us (32%)
  local copies, waits for them, and re-layouts  10.5 us (7%)
  other arithmetic  9.65 us (7%)
  matrix products  8.49 us (6%)
  starting transfers between devices  5.17 us (4%)
    all_to_all x1, blocking collectives, local(): lax.all_to_all(outgoing, 'exp', split_axis=0, concat_axis=0, tiled=True)  55.9 us
    all_to_all x1, waiting for transfers between devices, local(): lax.all_to_all(run_expert(arrived, gate_up, down_weight), 'exp', split_ax...  47.1 us
    gather x1, local copies, waits for them, and re-layouts, local(): jnp.take(returned_rows, target_slot, axis=0).astype(jnp.float32)  7.1 us
    all_to_all x1, starting transfers between devices, local(): lax.all_to_all(run_expert(arrived, gate_up, down_weight), 'exp', split_ax...  5.17 us
    reduce_sum x1, other arithmetic, local(): combined = jnp.sum(picked * routing_weight[:, :, None], axis=1)  3.86 us
    all_gather x1, blocking collectives, local(): lax.all_gather(key_rows, 'ctx', axis=1, tiled=True)  3.64 us
    all_gather x1, blocking collectives, local(): lax.all_gather(value_rows, 'ctx', axis=1, tiled=True)  3.63 us
  transfers between devices with their start and end apart: 1, of which 1 were waited for; matrix products, arithmetic and copies ran while one was open for 0% of the time, Pallas kernels for 0%

commit v1 on v0

--- a/solution.py
+++ b/solution.py
@@ -127,7 +127,19 @@
         "ts,td->sd", token_map, normed, preferred_element_type=jnp.float32
     ).astype(jnp.bfloat16)
     outgoing = outgoing.reshape(destinations, capacity, -1)
-    arrived = lax.all_to_all(outgoing, "exp", split_axis=0, concat_axis=0, tiled=True)
+    ways, here = (lax.axis_size("exp"), lax.axis_index("exp"))
+    width_2 = outgoing.shape[0] // ways
+    dims = list(outgoing.shape)
+    dims[0] = width_2
+    height = dims[0]
+    dims[0] = height * ways
+    full = jnp.zeros(dims, outgoing.dtype)
+    for mask in range(ways):
+        part = lax.dynamic_slice_in_dim(outgoing, (here ^ mask) * width_2, width_2, axis=0)
+        if mask:
+            part = lax.ppermute(part, "exp", [(d, d ^ mask) for d in range(ways)])
+        full = lax.dynamic_update_slice_in_dim(full, part, (here ^ mask) * height, axis=0)
+    arrived = full
     returned = lax.all_to_all(
         run_expert(arrived, gate_up, down_weight), "exp", split_axis=0, concat_axis=0, tiled=True
     )

time: 145 us -> 153 us (1.055)
  blocking collectives: 63.2 us -> 7.27 us
  waiting for transfers between devices: 47.1 us -> 83.8 us
  starting transfers between devices: 5.17 us -> 28.3 us
  local copies, waits for them, and re-layouts: 10.5 us -> 12.5 us
  other arithmetic: 9.65 us -> 11.6 us
    all_to_all x1 -> x0, blocking collectives: 55.9 us -> none  [local(): lax.all_to_all(outgoing, 'exp', split_axis=0, concat_axis=0, tiled=True)]
    ppermute x0 -> x15, waiting for transfers between devices: none -> 36.6 us  [local(): part = lax.ppermute(part, 'exp', [(d, d ^ mask) for d in range(ways)])]
    ppermute x0 -> x15, starting transfers between devices: none -> 22.1 us  [local(): part = lax.ppermute(part, 'exp', [(d, d ^ mask) for d in range(ways)])]
  transfers between devices with their start and end apart: 1 -> 16, of which waited for: 1 -> 10; matrix products, arithmetic and copies ran while one was open for 0% -> 0% of each run, Pallas kernels for 0% -> 0%
where the time goes in v1:
time: 153 us; the launch traced here: 152 us
  waiting for transfers between devices  83.8 us (55%)
  starting transfers between devices  28.3 us (18%)
  local copies, waits for them, and re-layouts  12.5 us (8%)
  other arithmetic  11.6 us (8%)
  matrix products  8.5 us (6%)
  blocking collectives  7.27 us (5%)
    all_to_all x1, waiting for transfers between devices, local(): lax.all_to_all(run_expert(arrived, gate_up, down_weight), 'exp', split_ax...  47.2 us
    ppermute x15, waiting for transfers between devices, local(): part = lax.ppermute(part, 'exp', [(d, d ^ mask) for d in range(ways)])  36.6 us
    ppermute x15, starting transfers between devices, local(): part = lax.ppermute(part, 'exp', [(d, d ^ mask) for d in range(ways)])  22.1 us
    gather x1, local copies, waits for them, and re-layouts, local(): jnp.take(returned_rows, target_slot, axis=0).astype(jnp.float32)  7.1 us
    all_to_all x1, starting transfers between devices, local(): lax.all_to_all(run_expert(arrived, gate_up, down_weight), 'exp', split_ax...  6.18 us
    reduce_sum x1, other arithmetic, local(): combined = jnp.sum(picked * routing_weight[:, :, None], axis=1)  3.86 us
    all_gather x1, blocking collectives, local(): lax.all_gather(key_rows, 'ctx', axis=1, tiled=True)  3.64 us
    all_gather x1, blocking collectives, local(): lax.all_gather(value_rows, 'ctx', axis=1, tiled=True)  3.63 us
  transfers between devices with their start and end apart: 16, of which 10 were waited for; matrix products, arithmetic and copies ran while one was open for 0% of the time, Pallas kernels for 0%

profile of v1, /device:TPU:11, one launch (start us, length us, event | category | flops | bytes accessed | tf_op | source)
XLA Modules:
  0.0 152.3 jit_solution(14142427187691413353)
XLA Ops:
  4.2 3.6 %all_gather.6 = bf16[1,128,256]{2,1,0:T(8,128)(2,1)S(1)} all-gather(bf16[1,64,256]{2,1,0:T(8,128)(2,1)} %param.12), channel_id=1, replica_groups=mesh['ctx'=2,'exp'=16] {'ctx'}, dimensions={1}, use_global_device_ids=true | all-gather | bytes 98304 | tf_op jit(solution)/shard_map/all_gather | solution.py:90
  9.1 3.6 %all_gather.7 = bf16[1,128,256]{2,1,0:T(8,128)(2,1)S(1)} all-gather(bf16[1,64,256]{2,1,0:T(8,128)(2,1)} %param.13), channel_id=1, replica_groups=mesh['ctx'=2,'exp'=16] {'ctx'}, dimensions={1}, use_global_device_ids=true | all-gather | bytes 98304 | tf_op jit(solution)/shard_map/all_gather | solution.py:91
  12.8 1.5 fusion.8
  21.0 1.7 %convolution_convert_fusion.1 = bf16[512,2048]{1,0:T(8,128)(2,1)S(1)} fusion(bf16[64,2048]{1,0:T(8,128)(2,1)S(1)} %bitcast.85, bf16[1,64,2048]{2,1,0:T(8,128)(2,1)} %param.10, f32[2048]{0:T(1024)S(1)} %copy-done.5, f32[64]{0:T(128)} %add_rsqrt_fusion, s32[64,512]{1,0:T(8,128)S(1)} %convert_reduce_fusion), kind=kOutput, calls=%fused_computation.5 | convolution fusion | flops 136085504 | bytes 2760960 | tf_op jit(solution)/shard_map/ts,td->sd/dot_general | solution.py:126
  23.3 3.0 %collective-permute-start = (bf16[1,32,2048]{2,1,0:T(8,128)(2,1)S(1)}, bf16[1,32,2048]{2,1,0:T(8,128)(2,1)S(1)}, u32[]{:S(2)}, u32[]{:S(2)}) collective-permute-start(bf16[1,32,2048]{2,1,0:T(8,128)(2,1)S(1)} %get-tuple-element.21), channel_id=1, source_target_pairs={{0,1},{1,0},{2,3},{3,2},{4,5},{5,4},{6,7},{7,6},{8,9},{9,8},{10,11... | collective-permute-start | bytes 393224 | tf_op jit(solution)/shard_map/ppermute | solution.py:140
  28.2 1.6 %collective-permute-start.4 = (bf16[1,32,2048]{2,1,0:T(8,128)(2,1)S(1)}, bf16[1,32,2048]{2,1,0:T(8,128)(2,1)S(1)}, u32[]{:S(2)}, u32[]{:S(2)}) collective-permute-start(bf16[1,32,2048]{2,1,0:T(8,128)(2,1)S(1)} %get-tuple-element.17), channel_id=1, source_target_pairs={{0,5},{1,4},{2,7},{3,6},{4,1},{5,0},{6,3},{7,2},{8,13},{9,12},{10,... | collective-permute-start | bytes 393224 | tf_op jit(solution)/shard_map/ppermute | solution.py:140
  29.9 1.5 collective-permute-done.1
  32.6 2.1 %collective-permute-done.2 = bf16[1,32,2048]{2,1,0:T(8,128)(2,1)S(1)} collective-permute-done((bf16[1,32,2048]{2,1,0:T(8,128)(2,1)S(1)}, bf16[1,32,2048]{2,1,0:T(8,128)(2,1)S(1)}, u32[]{:S(2)}, u32[]{:S(2)}) %collective-permute-start.2) | collective-permute-done | bytes 131104 | tf_op jit(solution)/shard_map/ppermute | solution.py:140
  34.7 2.3 %collective-permute-start.7 = (bf16[1,32,2048]{2,1,0:T(8,128)(2,1)S(1)}, bf16[1,32,2048]{2,1,0:T(8,128)(2,1)S(1)}, u32[]{:S(2)}, u32[]{:S(2)}) collective-permute-start(bf16[1,32,2048]{2,1,0:T(8,128)(2,1)S(1)} %get-tuple-element.14), channel_id=1, source_target_pairs={{0,8},{1,9},{2,10},{3,11},{4,12},{5,13},{6,14},{7,15},{8,0},{9,1},... | collective-permute-start | bytes 393224 | tf_op jit(solution)/shard_map/ppermute | solution.py:140
  37.2 2.3 %collective-permute-start.9 = (bf16[1,32,2048]{2,1,0:T(8,128)(2,1)S(1)}, bf16[1,32,2048]{2,1,0:T(8,128)(2,1)S(1)}, u32[]{:S(2)}, u32[]{:S(2)}) collective-permute-start(bf16[1,32,2048]{2,1,0:T(8,128)(2,1)S(1)} %get-tuple-element.12), channel_id=1, source_target_pairs={{0,10},{1,11},{2,8},{3,9},{4,14},{5,15},{6,12},{7,13},{8,2},{9,3},... | collective-permute-start | bytes 393224 | tf_op jit(solution)/shard_map/ppermute | solution.py:140
  39.6 7.3 %collective-permute-start.10 = (bf16[1,32,2048]{2,1,0:T(8,128)(2,1)S(1)}, bf16[1,32,2048]{2,1,0:T(8,128)(2,1)S(1)}, u32[]{:S(2)}, u32[]{:S(2)}) collective-permute-start(bf16[1,32,2048]{2,1,0:T(8,128)(2,1)S(1)} %get-tuple-element.11), channel_id=1, source_target_pairs={{0,11},{1,10},{2,9},{3,8},{4,15},{5,14},{6,13},{7,12},{8,3},{9,2},... | collective-permute-start | bytes 393224 | tf_op jit(solution)/shard_map/ppermute | solution.py:140
  48.4 11.3 %collective-permute-done.8 = bf16[1,32,2048]{2,1,0:T(8,128)(2,1)S(1)} collective-permute-done((bf16[1,32,2048]{2,1,0:T(8,128)(2,1)S(1)}, bf16[1,32,2048]{2,1,0:T(8,128)(2,1)S(1)}, u32[]{:S(2)}, u32[]{:S(2)}) %collective-permute-start.8) | collective-permute-done | bytes 131104 | tf_op jit(solution)/shard_map/ppermute | solution.py:140
  59.7 2.8 %collective-permute-done.9 = bf16[1,32,2048]{2,1,0:T(8,128)(2,1)S(1)} collective-permute-done((bf16[1,32,2048]{2,1,0:T(8,128)(2,1)S(1)}, bf16[1,32,2048]{2,1,0:T(8,128)(2,1)S(1)}, u32[]{:S(2)}, u32[]{:S(2)}) %collective-permute-start.9) | collective-permute-done | bytes 131104 | tf_op jit(solution)/shard_map/ppermute | solution.py:140
  63.4 4.6 %collective-permute-done.10 = bf16[1,32,2048]{2,1,0:T(8,128)(2,1)S(1)} collective-permute-done((bf16[1,32,2048]{2,1,0:T(8,128)(2,1)S(1)}, bf16[1,32,2048]{2,1,0:T(8,128)(2,1)S(1)}, u32[]{:S(2)}, u32[]{:S(2)}) %collective-permute-start.10) | collective-permute-done | bytes 131104 | tf_op jit(solution)/shard_map/ppermute | solution.py:140
  68.0 5.7 %collective-permute-done.11 = bf16[1,32,2048]{2,1,0:T(8,128)(2,1)S(1)} collective-permute-done((bf16[1,32,2048]{2,1,0:T(8,128)(2,1)S(1)}, bf16[1,32,2048]{2,1,0:T(8,128)(2,1)S(1)}, u32[]{:S(2)}, u32[]{:S(2)}) %collective-permute-start.11) | collective-permute-done | bytes 131104 | tf_op jit(solution)/shard_map/ppermute | solution.py:140
  73.8 2.9 %collective-permute-done.12 = bf16[1,32,2048]{2,1,0:T(8,128)(2,1)S(1)} collective-permute-done((bf16[1,32,2048]{2,1,0:T(8,128)(2,1)S(1)}, bf16[1,32,2048]{2,1,0:T(8,128)(2,1)S(1)}, u32[]{:S(2)}, u32[]{:S(2)}) %collective-permute-start.12) | collective-permute-done | bytes 131104 | tf_op jit(solution)/shard_map/ppermute | solution.py:140
  76.7 2.8 %collective-permute-done.13 = bf16[1,32,2048]{2,1,0:T(8,128)(2,1)S(1)} collective-permute-done((bf16[1,32,2048]{2,1,0:T(8,128)(2,1)S(1)}, bf16[1,32,2048]{2,1,0:T(8,128)(2,1)S(1)}, u32[]{:S(2)}, u32[]{:S(2)}) %collective-permute-start.13) | collective-permute-done | bytes 131104 | tf_op jit(solution)/shard_map/ppermute | solution.py:140
  79.5 2.8 %collective-permute-done.14 = bf16[1,32,2048]{2,1,0:T(8,128)(2,1)S(1)} collective-permute-done((bf16[1,32,2048]{2,1,0:T(8,128)(2,1)S(1)}, bf16[1,32,2048]{2,1,0:T(8,128)(2,1)S(1)}, u32[]{:S(2)}, u32[]{:S(2)}) %collective-permute-start.14) | collective-permute-done | bytes 131104 | tf_op jit(solution)/shard_map/ppermute | solution.py:140
  82.3 1.8 %fusion = f32[512,768]{1,0:T(8,128)S(1)} fusion(bf16[512,2048]{1,0:T(8,128)(2,1)S(1)} %bitcast.87, bf16[1,2048,768]{2,1,0:T(8,128)(2,1)S(1)} %copy-done), kind=kOutput, calls=%fused_computation.2 | convolution fusion | flops 1610612736 | bytes 6815744 | tf_op jit(solution)/shard_map/dot_general | solution.py:53
  84.1 2.6 %convolution_convert_fusion = bf16[512,2048]{1,0:T(8,128)(2,1)} fusion(bf16[1,384,2048]{2,1,0:T(8,128)(2,1)S(1)} %copy-done.8, f32[512,768]{1,0:T(8,128)S(1)} %fusion), kind=kOutput, calls=%fused_computation.4 | convolution fusion | flops 807534592 | bytes 5242880 | tf_op jit(solution)/shard_map/dot_general | solution.py:58
  86.7 6.2 %all-to-all-start = ((bf16[16,32,2048]{2,1,0:T(8,128)(2,1)}), bf16[16,32,2048]{2,1,0:T(8,128)(2,1)}, u32[]{:S(2)}, u32[]{:S(2)}) async-start(bf16[16,32,2048]{2,1,0:T(8,128)(2,1)} %bitcast.88), calls=%async_computation | async-start | bytes 4194304 | tf_op jit(solution)/shard_map/all_to_all | solution.py:143
  93.3 47.2 %all-to-all-done = bf16[16,32,2048]{2,1,0:T(8,128)(2,1)} async-done(((bf16[16,32,2048]{2,1,0:T(8,128)(2,1)}), bf16[16,32,2048]{2,1,0:T(8,128)(2,1)}, u32[]{:S(2)}, u32[]{:S(2)}) %all-to-all-start) | async-done | bytes 2097184 | tf_op jit(solution)/shard_map/all_to_all | solution.py:143
  140.5 7.1 %gather_fusion = bf16[512,2048]{1,0:T(8,128)(2,1)} fusion(bf16[512,2048]{1,0:T(8,128)(2,1)} %bitcast.15, s32[1024]{0:T(1024)S(1)} %pad_clamp_fusion), kind=kCustom, calls=%fused_computation | custom fusion | bytes 4196352 | tf_op jit(solution)/shard_map/jit(_take)/gather | solution.py:148
  147.6 3.9 %multiply_reduce_fusion = f32[64,2048]{1,0:T(8,128)S(1)} fusion(bf16[512,2048]{1,0:T(8,128)(2,1)} %gather_fusion, f32[64,8]{1,0:T(8,128)S(1)} %copy.61, pred[64,8]{1,0:T(8,128)(4,1)S(1)} %copy.58), kind=kLoop, calls=%fused_computation.1 | loop fusion | flops 4063232 | bytes 2624000 | tf_op jit(solution)/shard_map/reduce_sum | solution.py:152
  (92 shorter events, 19.5 us)
Async XLA Ops:
  0.0 82.3 %copy-start = (bf16[1,2048,768]{2,1,0:T(8,128)(2,1)S(1)}, bf16[1,2048,768]{2,1,0:T(8,128)(2,1)}, u32[]{:S(2)}) copy-start(bf16[1,2048,768]{2,1,0:T(8,128)(2,1)} %param.18) | copy-start | bytes 9437188
  12.8 3.2 %copy-start.1 = (bf16[1,64,2048]{2,1,0:T(8,128)(2,1)S(1)}, bf16[1,64,2048]{2,1,0:T(8,128)(2,1)}, u32[]{:S(2)}) copy-start(bf16[1,64,2048]{2,1,0:T(8,128)(2,1)} %param.10) | copy-start | bytes 786436
  14.3 3.9 %copy-start.6 = (s32[512]{0:T(512)S(1)}, s32[512]{0:T(512)}, u32[]{:S(2)}) copy-start(s32[512]{0:T(512)} %reshape_squeeze.15) | copy-start | bytes 6148
  14.3 4.2 %copy-start.3 = (s32[1,64,8]{1,2,0:T(8,128)S(1)}, s32[1,64,8]{1,2,0:T(8,128)}, u32[]{:S(2)}) copy-start(s32[1,64,8]{1,2,0:T(8,128)} %param.17) | copy-start | bytes 6148
  14.3 6.7 %copy-start.5 = (f32[2048]{0:T(1024)S(1)}, f32[2048]{0:T(1024)}, u32[]{:S(2)}) copy-start(f32[2048]{0:T(1024)} %param.15) | copy-start | bytes 24580
  23.3 6.5 %collective-permute-start = (bf16[1,32,2048]{2,1,0:T(8,128)(2,1)S(1)}, bf16[1,32,2048]{2,1,0:T(8,128)(2,1)S(1)}, u32[]{:S(2)}, u32[]{:S(2)}) collective-permute-start(bf16[1,32,2048]{2,1,0:T(8,128)(2,1)S(1)} %get-tuple-element.21), channel_id=1, source_target_pairs={{0,1},{1,0},{2,3},{3,2},{4,5},{5,4},{6,7},{7,6},{8,9},{9,8},{10,11... | collective-permute-start | bytes 393224 | tf_op jit(solution)/shard_map/ppermute | solution.py:140
  26.4 5.0 %collective-permute-start.1 = (bf16[1,32,2048]{2,1,0:T(8,128)(2,1)S(1)}, bf16[1,32,2048]{2,1,0:T(8,128)(2,1)S(1)}, u32[]{:S(2)}, u32[]{:S(2)}) collective-permute-start(bf16[1,32,2048]{2,1,0:T(8,128)(2,1)S(1)} %get-tuple-element.20), channel_id=1, source_target_pairs={{0,2},{1,3},{2,0},{3,1},{4,6},{5,7},{6,4},{7,5},{8,10},{9,11},{10,... | collective-permute-start | bytes 393224 | tf_op jit(solution)/shard_map/ppermute | solution.py:140
  26.6 8.1 %collective-permute-start.2 = (bf16[1,32,2048]{2,1,0:T(8,128)(2,1)S(1)}, bf16[1,32,2048]{2,1,0:T(8,128)(2,1)S(1)}, u32[]{:S(2)}, u32[]{:S(2)}) collective-permute-start(bf16[1,32,2048]{2,1,0:T(8,128)(2,1)S(1)} %get-tuple-element.19), channel_id=1, source_target_pairs={{0,3},{1,2},{2,1},{3,0},{4,7},{5,6},{6,5},{7,4},{8,11},{9,10},{10,... | collective-permute-start | bytes 393224 | tf_op jit(solution)/shard_map/ppermute | solution.py:140
  28.1 8.9 %collective-permute-start.3 = (bf16[1,32,2048]{2,1,0:T(8,128)(2,1)S(1)}, bf16[1,32,2048]{2,1,0:T(8,128)(2,1)S(1)}, u32[]{:S(2)}, u32[]{:S(2)}) collective-permute-start(bf16[1,32,2048]{2,1,0:T(8,128)(2,1)S(1)} %get-tuple-element.18), channel_id=1, source_target_pairs={{0,4},{1,5},{2,6},{3,7},{4,0},{5,1},{6,2},{7,3},{8,12},{9,13},{10,... | collective-permute-start | bytes 393224 | tf_op jit(solution)/shard_map/ppermute | solution.py:140
  28.2 8.9 %collective-permute-start.4 = (bf16[1,32,2048]{2,1,0:T(8,128)(2,1)S(1)}, bf16[1,32,2048]{2,1,0:T(8,128)(2,1)S(1)}, u32[]{:S(2)}, u32[]{:S(2)}) collective-permute-start(bf16[1,32,2048]{2,1,0:T(8,128)(2,1)S(1)} %get-tuple-element.17), channel_id=1, source_target_pairs={{0,5},{1,4},{2,7},{3,6},{4,1},{5,0},{6,3},{7,2},{8,13},{9,12},{10,... | collective-permute-start | bytes 393224 | tf_op jit(solution)/shard_map/ppermute | solution.py:140
  29.9 9.7 %collective-permute-start.5 = (bf16[1,32,2048]{2,1,0:T(8,128)(2,1)S(1)}, bf16[1,32,2048]{2,1,0:T(8,128)(2,1)S(1)}, u32[]{:S(2)}, u32[]{:S(2)}) collective-permute-start(bf16[1,32,2048]{2,1,0:T(8,128)(2,1)S(1)} %get-tuple-element.16), channel_id=1, source_target_pairs={{0,6},{1,7},{2,4},{3,5},{4,2},{5,3},{6,0},{7,1},{8,14},{9,15},{10,... | collective-permute-start | bytes 393224 | tf_op jit(solution)/shard_map/ppermute | solution.py:140
  31.3 15.5 %collective-permute-start.6 = (bf16[1,32,2048]{2,1,0:T(8,128)(2,1)S(1)}, bf16[1,32,2048]{2,1,0:T(8,128)(2,1)S(1)}, u32[]{:S(2)}, u32[]{:S(2)}) collective-permute-start(bf16[1,32,2048]{2,1,0:T(8,128)(2,1)S(1)} %get-tuple-element.15), channel_id=1, source_target_pairs={{0,7},{1,6},{2,5},{3,4},{4,3},{5,2},{6,1},{7,0},{8,15},{9,14},{10,... | collective-permute-start | bytes 393224 | tf_op jit(solution)/shard_map/ppermute | solution.py:140
  34.7 13.6 %collective-permute-start.7 = (bf16[1,32,2048]{2,1,0:T(8,128)(2,1)S(1)}, bf16[1,32,2048]{2,1,0:T(8,128)(2,1)S(1)}, u32[]{:S(2)}, u32[]{:S(2)}) collective-permute-start(bf16[1,32,2048]{2,1,0:T(8,128)(2,1)S(1)} %get-tuple-element.14), channel_id=1, source_target_pairs={{0,8},{1,9},{2,10},{3,11},{4,12},{5,13},{6,14},{7,15},{8,0},{9,1},... | collective-permute-start | bytes 393224 | tf_op jit(solution)/shard_map/ppermute | solution.py:140
  37.0 22.7 %collective-permute-start.8 = (bf16[1,32,2048]{2,1,0:T(8,128)(2,1)S(1)}, bf16[1,32,2048]{2,1,0:T(8,128)(2,1)S(1)}, u32[]{:S(2)}, u32[]{:S(2)}) collective-permute-start(bf16[1,32,2048]{2,1,0:T(8,128)(2,1)S(1)} %get-tuple-element.13), channel_id=1, source_target_pairs={{0,9},{1,8},{2,11},{3,10},{4,13},{5,12},{6,15},{7,14},{8,1},{9,0},... | collective-permute-start | bytes 393224 | tf_op jit(solution)/shard_map/ppermute | solution.py:140
  37.2 25.3 %collective-permute-start.9 = (bf16[1,32,2048]{2,1,0:T(8,128)(2,1)S(1)}, bf16[1,32,2048]{2,1,0:T(8,128)(2,1)S(1)}, u32[]{:S(2)}, u32[]{:S(2)}) collective-permute-start(bf16[1,32,2048]{2,1,0:T(8,128)(2,1)S(1)} %get-tuple-element.12), channel_id=1, source_target_pairs={{0,10},{1,11},{2,8},{3,9},{4,14},{5,15},{6,12},{7,13},{8,2},{9,3},... | collective-permute-start | bytes 393224 | tf_op jit(solution)/shard_map/ppermute | solution.py:140
  39.6 28.4 %collective-permute-start.10 = (bf16[1,32,2048]{2,1,0:T(8,128)(2,1)S(1)}, bf16[1,32,2048]{2,1,0:T(8,128)(2,1)S(1)}, u32[]{:S(2)}, u32[]{:S(2)}) collective-permute-start(bf16[1,32,2048]{2,1,0:T(8,128)(2,1)S(1)} %get-tuple-element.11), channel_id=1, source_target_pairs={{0,11},{1,10},{2,9},{3,8},{4,15},{5,14},{6,13},{7,12},{8,3},{9,2},... | collective-permute-start | bytes 393224 | tf_op jit(solution)/shard_map/ppermute | solution.py:140
  46.9 26.9 %collective-permute-start.11 = (bf16[1,32,2048]{2,1,0:T(8,128)(2,1)S(1)}, bf16[1,32,2048]{2,1,0:T(8,128)(2,1)S(1)}, u32[]{:S(2)}, u32[]{:S(2)}) collective-permute-start(bf16[1,32,2048]{2,1,0:T(8,128)(2,1)S(1)} %get-tuple-element.10), channel_id=1, source_target_pairs={{0,12},{1,13},{2,14},{3,15},{4,8},{5,9},{6,10},{7,11},{8,4},{9,5},... | collective-permute-start | bytes 393224 | tf_op jit(solution)/shard_map/ppermute | solution.py:140
  48.3 28.4 %collective-permute-start.12 = (bf16[1,32,2048]{2,1,0:T(8,128)(2,1)S(1)}, bf16[1,32,2048]{2,1,0:T(8,128)(2,1)S(1)}, u32[]{:S(2)}, u32[]{:S(2)}) collective-permute-start(bf16[1,32,2048]{2,1,0:T(8,128)(2,1)S(1)} %get-tuple-element.9), channel_id=1, source_target_pairs={{0,13},{1,12},{2,15},{3,14},{4,9},{5,8},{6,11},{7,10},{8,5},{9,4},... | collective-permute-start | bytes 393224 | tf_op jit(solution)/shard_map/ppermute | solution.py:140
  59.7 19.8 %collective-permute-start.13 = (bf16[1,32,2048]{2,1,0:T(8,128)(2,1)S(1)}, bf16[1,32,2048]{2,1,0:T(8,128)(2,1)S(1)}, u32[]{:S(2)}, u32[]{:S(2)}) collective-permute-start(bf16[1,32,2048]{2,1,0:T(8,128)(2,1)S(1)} %get-tuple-element.8), channel_id=1, source_target_pairs={{0,14},{1,15},{2,12},{3,13},{4,10},{5,11},{6,8},{7,9},{8,6},{9,7},... | collective-permute-start | bytes 393224 | tf_op jit(solution)/shard_map/ppermute | solution.py:140
  62.5 19.8 %collective-permute-start.14 = (bf16[1,32,2048]{2,1,0:T(8,128)(2,1)S(1)}, bf16[1,32,2048]{2,1,0:T(8,128)(2,1)S(1)}, u32[]{:S(2)}, u32[]{:S(2)}) collective-permute-start(bf16[1,32,2048]{2,1,0:T(8,128)(2,1)S(1)} %get-tuple-element.7), channel_id=1, source_target_pairs={{0,15},{1,14},{2,13},{3,12},{4,11},{5,10},{6,9},{7,8},{8,7},{9,6},... | collective-permute-start | bytes 393224 | tf_op jit(solution)/shard_map/ppermute | solution.py:140
  86.7 6.4 %copy-start.7 = (pred[64,8]{0,1:T(8,128)(4,1)S(1)}, pred[64,8]{0,1:T(8,128)(4,1)}, u32[]{:S(2)}) copy-start(pred[64,8]{0,1:T(8,128)(4,1)} %get-tuple-element.5) | copy-start | bytes 1540
  86.7 6.5 %copy-start.4 = (f32[1,64,8]{1,2,0:T(8,128)S(1)}, f32[1,64,8]{1,2,0:T(8,128)}, u32[]{:S(2)}) copy-start(f32[1,64,8]{1,2,0:T(8,128)} %param.16) | copy-start | bytes 6148
  86.7 53.8 %all-to-all-start = ((bf16[16,32,2048]{2,1,0:T(8,128)(2,1)}), bf16[16,32,2048]{2,1,0:T(8,128)(2,1)}, u32[]{:S(2)}, u32[]{:S(2)}) async-start(bf16[16,32,2048]{2,1,0:T(8,128)(2,1)} %bitcast.88), calls=%async_computation | async-start | bytes 4194304 | tf_op jit(solution)/shard_map/all_to_all | solution.py:143
  147.6 3.9 %copy-start.2 = (bf16[1,64,2048]{2,1,0:T(8,128)(2,1)S(1)}, bf16[1,64,2048]{2,1,0:T(8,128)(2,1)}, u32[]{:S(2)}) copy-start(bf16[1,64,2048]{2,1,0:T(8,128)(2,1)} %param.10) | copy-start | bytes 786436
  (1 other events, 1.8 us)
